TPU v7x, 32 devices: a whole 2x2x4 slice. The times are simulated.
32 devices in a mesh: grp: 8 (over z, core), rep: 4 (over y, x).
Axes of the slice: x: 2, y: 2, z: 4, core: 2. Of those that a mesh axis runs over, the one named last changes fastest.
Arguments:
- queries: bfloat16 [12288, 2560], P(('grp', 'rep')), may hold values from -60 to 60
- passages: bfloat16 [65536, 2560], P(('grp', 'rep')), may hold values from -60 to 60
- block_valid_counts: int32 [512], P(('grp', 'rep')), may hold values from 16 to 128
- positive_index: int32 [12288], P(('grp', 'rep')), may hold values from 0 to 2047, as said below
- neg_blocks: int32 [32, 12], P(('grp', 'rep')), may hold values from 0 to 511, as said below
- query_weights: float32 [12288], P(('grp', 'rep')), may hold values from 0.3 to 10
Outputs:
- query_loss: float32 [12288], P(('grp', 'rep'))
- mean_loss: float32 [], replicated
Inputs may be any that keep to these rules, and one draw needn't show every extreme that they name: `neg_blocks`: row g lists 12 distinct blocks, all owned by query groups with the same rep index as group g and another grp index; at most 2 of them belong to one group, and some group gives exactly 2 in every row. `positive_index`: always a valid row of one of the query's own group's blocks.
All inputs are finite; a program needn't handle non-finite values.
Results may differ from a plain program's by a relative error of at most 0.0003.
Values may be sent and summed in bfloat16 or wider, within the bound.
A program may use at most 256 MiB of HBM per device.

v0:
```python
import jax
import jax.numpy as jnp
from jax import lax
from jax.sharding import PartitionSpec as P

CAP = 2


inverse_softmax_sharpness = 20.0
norm_epsilon = 1e-06


def normalize(rows):
    values = rows.astype(jnp.float32)
    scale = lax.rsqrt(jnp.sum(values * values, axis=-1, keepdims=True) + norm_epsilon)
    return (values * scale).astype(jnp.bfloat16)


def local(queries, passages, block_valid_counts, positive_index, neg_blocks, query_weights):
    group_count = lax.axis_size("grp")
    replica_count = lax.axis_size("rep")
    local_rows = passages.shape[0]
    blocks_here = block_valid_counts.shape[0]
    block_rows = local_rows // blocks_here
    feature_width = passages.shape[1]
    question_unit_vectors = normalize(queries)
    document_unit_vectors = normalize(passages)
    row_valid = jnp.arange(local_rows, dtype=jnp.int32) % block_rows < jnp.repeat(
        block_valid_counts, block_rows
    )
    shared_pool_similarity = (
        lax.dot_general(
            question_unit_vectors,
            document_unit_vectors,
            (((1,), (1,)), ((), ())),
            preferred_element_type=jnp.float32,
        )
        * inverse_softmax_sharpness
    )
    local_total = jnp.sum(
        jnp.where(row_valid[None, :], jnp.exp(shared_pool_similarity), 0.0), axis=1
    )
    positive_score = jnp.take_along_axis(shared_pool_similarity, positive_index[:, None], axis=1)[
        :, 0
    ]
    wanted = neg_blocks[0]
    owner_device = wanted // blocks_here
    owner_group = owner_device // replica_count
    local_block = wanted % blocks_here
    listed = wanted.shape[0]
    same_owner = owner_group[:, None] == owner_group[None, :]
    earlier_slot = jnp.arange(listed)[:, None] > jnp.arange(listed)[None, :]
    slot_rank = jnp.sum(jnp.logical_and(same_owner, earlier_slot), axis=1)
    requests = (
        jnp.full((group_count, CAP), -1, jnp.int32).at[owner_group, slot_rank].set(local_block)
    )
    incoming = lax.all_to_all(requests, "grp", split_axis=0, concat_axis=0, tiled=True)
    requested = incoming >= 0
    safe_block = jnp.maximum(incoming, 0)
    matches = safe_block[:, :, None] == jnp.arange(blocks_here, dtype=jnp.int32)[None, None, :]
    slot_counts = jnp.where(
        requested, jnp.sum(jnp.where(matches, block_valid_counts[None, None, :], 0), axis=2), 0
    )
    unit_blocks = document_unit_vectors.reshape(blocks_here, block_rows, feature_width)
    picked = unit_blocks[safe_block]
    arrived = lax.all_to_all(picked, "grp", split_axis=0, concat_axis=0, tiled=True)
    kept_counts = lax.all_to_all(slot_counts, "grp", split_axis=0, concat_axis=0, tiled=True)
    similarity = (
        jnp.einsum(
            "qd,skrd->kqsr", question_unit_vectors, arrived, preferred_element_type=jnp.float32
        )
        * inverse_softmax_sharpness
    )
    live_rows = jnp.arange(block_rows, dtype=jnp.int32)[None, None, :] < kept_counts[:, :, None]
    live_rows = jnp.transpose(live_rows, (1, 0, 2))[:, None]
    slot_totals = jnp.sum(jnp.where(live_rows, jnp.exp(similarity), 0.0), axis=(2, 3))
    hard_total = jnp.sum(slot_totals, axis=0)
    query_loss = jnp.log(local_total + hard_total) - positive_score
    weighted_sum, weight_sum = lax.psum(
        (jnp.sum(query_weights * query_loss), jnp.sum(query_weights)), ("grp", "rep")
    )
    return (query_loss, weighted_sum / weight_sum)


def solution(mesh):
    in_specs = (
        P(("grp", "rep"), None),
        P(("grp", "rep"), None),
        P(("grp", "rep")),
        P(("grp", "rep")),
        P(("grp", "rep"), None),
        P(("grp", "rep")),
    )
    out_specs = (P(("grp", "rep")), P())
    return jax.shard_map(local, mesh=mesh, in_specs=in_specs, out_specs=out_specs, check_vma=False)
```

profile of v0, /device:TPU:0, one launch (start us, length us, event | category | flops | bytes accessed | tf_op | source)
XLA Modules:
  0.0 323.6 jit_solution(4056627843211229691)
XLA Ops:
  0.6 0.7 fusion.21
  1.3 0.7 and_select_fusion
  2.0 0.2 convert_reduce_fusion
  2.2 0.7 fusion.22
  2.8 1.1 scatter_fusion
  4.0 0.7 copy.22
  4.6 6.4 %all-to-all-start = ((s32[8,1,2]{2,1,0:T(1,128)}), s32[8,1,2]{2,1,0:T(1,128)S(1)}, u32[]{:S(2)}, u32[]{:S(2)}) async-start(s32[8,1,2]{2,1,0:T(1,128)} %copy.22), calls=%async_computation | async-start | bytes 8192 | tf_op jit(solution)/shard_map/all_to_all | solution.py:57
  11.0 6.2 %fusion = f32[2048]{0:T(1024)S(1)} fusion(bf16[2048,2560]{1,0:T(8,128)(2,1)} %param.7), kind=kLoop, calls=%fused_computation.5 | loop fusion | flops 15726592 | bytes 10493952 | tf_op jit(solution)/shard_map/reduce_sum | solution.py:15
  17.2 0.7 copy-done
  17.9 5.5 %fusion.1 = bf16[2048,2560]{1,0:T(8,128)(2,1)} fusion(bf16[2048,2560]{1,0:T(8,128)(2,1)S(1)} %copy-done, f32[2048]{0:T(1024)S(1)} %add_rsqrt_fusion), kind=kLoop, calls=%fused_computation.6 | loop fusion | flops 15728640 | bytes 20979712 | tf_op jit(solution)/shard_map/convert_element_type | solution.py:16
  23.4 0.0 all-to-all-done
  23.4 0.1 copy.23
  23.5 0.2 select_reduce_fusion.1
  23.8 0.7 copy.25
  24.4 0.1 copy.28
  24.5 0.1 reshape.238
  24.6 5.1 %all-to-all-start.1 = ((s32[8,1,2]{2,1,0:T(1,128)}), s32[8,1,2]{2,1,0:T(1,128)S(1)}, u32[]{:S(2)}, u32[]{:S(2)}) async-start(s32[8,1,2]{2,1,0:T(1,128)} %copy.25), calls=%async_computation.1 | async-start | bytes 8192 | tf_op jit(solution)/shard_map/all_to_all | solution.py:67
  29.7 9.5 %gather_fusion = bf16[16,128,2560]{2,1,0:T(8,128)(2,1)} fusion(bf16[16,128,2560]{2,1,0:T(8,128)(2,1)} %bitcast.68, s32[1024]{0:T(1024)S(1)} %pad_clamp_fusion), kind=kCustom, calls=%fused_computation | custom fusion | bytes 20971584 | tf_op jit(solution)/shard_map/gather | solution.py:65
  39.2 0.0 all-to-all-done.1
  39.2 5.3 %all-to-all-start.2 = ((bf16[8,2,128,2560]{3,2,1,0:T(8,128)(2,1)}), bf16[8,2,128,2560]{3,2,1,0:T(8,128)(2,1)}, u32[]{:S(2)}, u32[]{:S(2)}) async-start(bf16[8,2,128,2560]{3,2,1,0:T(8,128)(2,1)} %bitcast.69), calls=%async_computation.2 | async-start | bytes 20971520 | tf_op jit(solution)/shard_map/all_to_all | solution.py:66
  44.6 0.1 fusion.11
  44.7 0.5 fusion.2
  45.2 9.9 %select_reduce_fusion = (f32[384]{0:T(512)S(1)}, f32[384,2048]{1,0:T(8,128)}) fusion(pred[2048]{0:T(1024)(128)(4,1)S(1)} %fusion.11, bf16[2048,2560]{1,0:T(8,128)(2,1)} %fusion.1, bf16[384,2560]{1,0:T(8,128)(2,1)S(1)} %copy-done.1, f32[384]{0:T(512)S(1)} %add_rsqrt_fusion.1), kind=kOutput, calls=%fused_computation.13 | convolution fusion | flops 4031839744 | bytes 15602688 | tf_op jit(solution)/shard_map/dot_general | solution.py:32
  55.1 5.1 %gather_fusion.1 = f32[384]{0:T(512)S(1)} fusion(f32[384,2048]{1,0:T(8,128)} %get-tuple-element.12, s32[384]{0:T(512)S(1)} %fusion.19), kind=kCustom, calls=%fused_computation.1 | custom fusion | bytes 6144 | tf_op jit(solution)/shard_map/jit(take_along_axis)/gather | solution.py:43
  60.2 0.1 copy.26
  60.3 0.1 copy.27
  60.4 0.1 iota_compare_fusion.2
  60.4 0.0 copy-start.4
  60.5 213.0 %all-to-all-done.2 = bf16[8,2,128,2560]{3,2,1,0:T(8,128)(2,1)} async-done(((bf16[8,2,128,2560]{3,2,1,0:T(8,128)(2,1)}), bf16[8,2,128,2560]{3,2,1,0:T(8,128)(2,1)}, u32[]{:S(2)}, u32[]{:S(2)}) %all-to-all-start.2) | async-done | bytes 10485792 | tf_op jit(solution)/shard_map/all_to_all | solution.py:66
  273.4 8.5 %fusion.4 = f32[384]{0:T(512)S(1)} fusion(pred[2,8,128]{2,0,1:T(4,128)(4,1)S(1)} %iota_compare_fusion.2, bf16[8,2,128,2560]{3,2,1,0:T(8,128)(2,1)} %all-to-all-done.2, bf16[384,2560]{1,0:T(8,128)(2,1)S(1)} %copy-done.1, f32[384]{0:T(512)S(1)} %add_rsqrt_fusion.1), kind=kOutput, calls=%fused_computation.12 | convolution fusion | flops 4031839744 | bytes 12456960 | tf_op jit(solution)/shard_map/qd,skrd->kqsr/dot_general | solution.py:69
  281.9 1.3 fusion.24
  283.2 38.1 %all-reduce = (f32[]{:T(128)}, f32[]{:T(128)}) all-reduce(f32[]{:T(128)} %get-tuple-element.3, f32[]{:T(128)} %get-tuple-element.2), channel_id=1, replica_groups=mesh['grp'=8,'rep'=4] {'grp','rep'}, use_global_device_ids=true, to_apply=%region_8.9 | all-reduce | flops 2 | bytes 16 | tf_op jit(solution)/shard_map/psum | solution.py:79
  (19 shorter events, 0.1 us)
Async XLA Ops:
  4.6 18.8 %all-to-all-start = ((s32[8,1,2]{2,1,0:T(1,128)}), s32[8,1,2]{2,1,0:T(1,128)S(1)}, u32[]{:S(2)}, u32[]{:S(2)}) async-start(s32[8,1,2]{2,1,0:T(1,128)} %copy.22), calls=%async_computation | async-start | bytes 8192 | tf_op jit(solution)/shard_map/all_to_all | solution.py:57
  11.0 7.0 %copy-start = (bf16[2048,2560]{1,0:T(8,128)(2,1)S(1)}, bf16[2048,2560]{1,0:T(8,128)(2,1)}, u32[]{:S(2)}) copy-start(bf16[2048,2560]{1,0:T(8,128)(2,1)} %param.7) | copy-start | bytes 31457284
  17.9 5.6 %copy-start.3 = (s32[16]{0:T(128)S(1)}, s32[16]{0:T(128)}, u32[]{:S(2)}) copy-start(s32[16]{0:T(128)} %param.8) | copy-start | bytes 196
  24.6 14.6 %all-to-all-start.1 = ((s32[8,1,2]{2,1,0:T(1,128)}), s32[8,1,2]{2,1,0:T(1,128)S(1)}, u32[]{:S(2)}, u32[]{:S(2)}) async-start(s32[8,1,2]{2,1,0:T(1,128)} %copy.25), calls=%async_computation.1 | async-start | bytes 8192 | tf_op jit(solution)/shard_map/all_to_all | solution.py:67
  39.2 5.3 %copy-start.2 = (s32[384]{0:T(512)S(1)}, s32[384]{0:T(512)}, u32[]{:S(2)}) copy-start(s32[384]{0:T(512)} %param.9) | copy-start | bytes 4612
  39.2 5.5 %copy-start.1 = (bf16[384,2560]{1,0:T(8,128)(2,1)S(1)}, bf16[384,2560]{1,0:T(8,128)(2,1)}, u32[]{:S(2)}) copy-start(bf16[384,2560]{1,0:T(8,128)(2,1)} %param.6) | copy-start | bytes 5898244
  39.2 234.2 %all-to-all-start.2 = ((bf16[8,2,128,2560]{3,2,1,0:T(8,128)(2,1)}), bf16[8,2,128,2560]{3,2,1,0:T(8,128)(2,1)}, u32[]{:S(2)}, u32[]{:S(2)}) async-start(bf16[8,2,128,2560]{3,2,1,0:T(8,128)(2,1)} %bitcast.69), calls=%async_computation.2 | async-start | bytes 20971520 | tf_op jit(solution)/shard_map/all_to_all | solution.py:66
  60.4 221.5 %copy-start.4 = (f32[384]{0:T(512)S(1)}, f32[384]{0:T(512)}, u32[]{:S(2)}) copy-start(f32[384]{0:T(512)} %param.11) | copy-start | bytes 4612
where the time goes:
time: 325 us; the launch traced here: 324 us
  waiting for transfers between devices  213 us (66%)
  blocking collectives  38.1 us (12%)
  matrix products  18.4 us (6%)
  local copies, waits for them, and re-layouts  18.2 us (6%)
  starting transfers between devices  16.7 us (5%)
  other arithmetic  16.1 us (5%)
    all_to_all x1, waiting for transfers between devices, local(): lax.all_to_all(picked, 'grp', split_axis=0, concat_axis=0, tiled=True)  213 us
    psum x1, blocking collectives, local(): lax.psum((jnp.sum(query_weights * query_loss), jnp.sum(query_weights)), (...  38.1 us
    dot_general x1, matrix products, local(): lax.dot_general(question_unit_vectors, document_unit_vectors, (((1,), (1,...  9.91 us
    gather x1, local copies, waits for them, and re-layouts, local(): picked = unit_blocks[safe_block]  9.52 us
    dot_general x1, matrix products, local(): jnp.einsum('qd,skrd->kqsr', question_unit_vectors, arrived, preferred_ele...  8.48 us
    reduce_sum x2, other arithmetic, normalize(): jnp.sum(values * values, axis=-1, keepdims=True) + norm_epsilon  6.69 us
  transfers between devices with their start and end apart: 3, of which 1 were waited for; matrix products, arithmetic and copies ran while one was open for 11% of the time, Pallas kernels for 0%

commit v1 on v0

v1 whole, which is shorter than its diff:
```python
import functools

import jax
import jax.numpy as jnp
from jax import lax
from jax.experimental import pallas as pl
from jax.experimental.pallas import tpu as pltpu
from jax.sharding import PartitionSpec as P

sharpness = 20.0
norm_epsilon = 1e-06
LANES = 128
MESH = pl.DeviceIdType.MESH


def unit(rows):
    values = rows.astype(jnp.float32)
    scale = lax.rsqrt(jnp.sum(values * values, axis=-1, keepdims=True) + norm_epsilon)
    return (values * scale).astype(jnp.bfloat16)


def scores(passage_rows, query_rows):
    return (
        lax.dot_general(
            passage_rows,
            query_rows,
            (((1,), (1,)), ((), ())),
            preferred_element_type=jnp.float32,
        )
        * sharpness
    )


def kernel(
    G,
    REP,
    counts,
    neg,
    positive,
    weights,
    q_hbm,
    p_hbm,
    loss_ref,
    mean_ref,
    qall,
    pun,
    qown,
    qsub,
    wants_out,
    wants_in,
    wants_s,
    table,
    tot_out,
    tot_in,
    part_out,
    part_grp,
    sum_out,
    part_rep,
    q_sem,
    p_sem,
    want_send,
    want_recv,
    smem_sem,
    right_send,
    left_send,
    side_send,
    recv,
    tot_send,
    tot_recv,
    grp_send,
    grp_recv,
    rep_send,
    rep_recv,
):
    g = lax.axis_index("grp")
    r = lax.axis_index("rep")
    blocks, BR, D = p_hbm.shape
    QG = q_hbm.shape[0]
    listed = neg.shape[1]
    R = LANES
    NS = QG // R
    C = G // 2
    z = g // 2
    c = g % 2
    side = 2 * z + 1 - c

    barrier = pltpu.get_barrier_semaphore()
    for k in range(1, G):
        pl.semaphore_signal(
            barrier, inc=1, device_id={"grp": lax.rem(g + k, G)}, device_id_type=MESH
        )
    for k in range(1, REP):
        pl.semaphore_signal(
            barrier, inc=1, device_id={"rep": lax.rem(r + k, REP)}, device_id_type=MESH
        )

    own_copy = pltpu.make_async_copy(q_hbm, qown, q_sem)
    own_copy.start()

    def passage_copy(b):
        return pltpu.make_async_copy(p_hbm.at[b], pun.at[b], p_sem.at[b])

    @pl.loop(0, blocks)
    def _(b):
        passage_copy(b).start()

    wants_out[...] = jnp.zeros_like(wants_out)
    wants_out[0:1, 0:listed] = neg[...]
    pl.semaphore_wait(barrier, G - 1 + REP - 1)

    def want_copy(k):
        return pltpu.make_async_remote_copy(
            wants_out,
            wants_in.at[g],
            want_send.at[k],
            want_recv.at[g],
            device_id={"grp": lax.rem(g + k, G)},
            device_id_type=MESH,
        )

    def want_arrival(k):
        src = lax.rem(g + k, G)
        return pltpu.make_async_remote_copy(
            wants_out,
            wants_in.at[src],
            want_send.at[k],
            want_recv.at[src],
            device_id={"grp": src},
            device_id_type=MESH,
        )

    def own_piece(j, sem, target):
        rows = pl.ds(pl.multiple_of(j * R, R), R)
        return pltpu.make_async_remote_copy(
            q_hbm.at[rows],
            qall.at[g, rows],
            sem.at[g, j],
            recv.at[g, j],
            device_id={"grp": target},
            device_id_type=MESH,
        )

    def piece(gq, j, sem, target):
        rows = pl.ds(pl.multiple_of(j * R, R), R)
        return pltpu.make_async_remote_copy(
            qall.at[gq, rows],
            qall.at[gq, rows],
            sem.at[gq, j],
            recv.at[gq, j],
            device_id={"grp": target},
            device_id_type=MESH,
        )

    for k in range(1, G):
        want_copy(k).start()

    @pl.loop(0, NS)
    def _(j):
        @pl.when(z + 1 < C)
        def _():
            own_piece(j, right_send, g + 2).start()

        @pl.when(z > 0)
        def _():
            own_piece(j, left_send, g - 2).start()

        own_piece(j, side_send, side).start()

    own_copy.wait()

    @pl.loop(0, NS)
    def _(j):
        rows = pl.ds(pl.multiple_of(j * R, R), R)
        qown[rows, :] = unit(qown[rows, :])

    def own_block(b, carry):
        total, pos = carry
        passage_copy(b).wait()
        pun[b] = unit(pun[b])
        st = scores(pun[b], qown[...])
        row = lax.broadcasted_iota(jnp.int32, st.shape, 0)
        live = row < counts[b]
        total = total + jnp.sum(jnp.where(live, jnp.exp(st), 0.0), axis=0, keepdims=True)
        hit = row + b * BR == positive[...]
        pos = pos + jnp.sum(jnp.where(hit, st, 0.0), axis=0, keepdims=True)
        return total, pos

    zero = jnp.zeros((1, QG), jnp.float32)
    local_total, pos = lax.fori_loop(0, blocks, own_block, (zero, zero))
    tot_in[g, 0:1, :] = local_total

    for k in range(1, G):
        want_arrival(k).wait_recv()
    wants_in[g] = wants_out[...]
    to_smem = pltpu.make_async_copy(wants_in, wants_s, smem_sem)
    to_smem.start()
    to_smem.wait()
    me = g * REP + r

    @pl.loop(0, G)
    def _(gq):
        found = jnp.int32(0)
        first = jnp.int32(0)
        second = jnp.int32(0)
        for i in range(listed):
            w = wants_s[gq, 0, i]
            local = w - me * blocks
            mine = jnp.logical_and(local >= 0, local < blocks)
            first = jnp.where(jnp.logical_and(mine, found == 0), local, first)
            second = jnp.where(jnp.logical_and(mine, found == 1), local, second)
            found = found + mine.astype(jnp.int32)
        table[gq, 0] = first
        table[gq, 1] = jnp.where(found > 0, counts[first], 0)
        table[gq, 2] = second
        table[gq, 3] = jnp.where(found > 1, counts[second], 0)

    def tot_copy(gq):
        return pltpu.make_async_remote_copy(
            tot_out.at[gq],
            tot_in.at[g],
            tot_send.at[gq],
            tot_recv.at[g],
            device_id={"grp": gq},
            device_id_type=MESH,
        )

    def tot_arrival(src):
        return pltpu.make_async_remote_copy(
            tot_out.at[src],
            tot_in.at[src],
            tot_send.at[src],
            tot_recv.at[src],
            device_id={"grp": src},
            device_id_type=MESH,
        )

    def hard(gq, j):
        rows = pl.ds(pl.multiple_of(j * R, R), R)
        qsub[...] = unit(qall[gq, rows, :])
        total = jnp.zeros((1, R), jnp.float32)
        for slot in range(2):
            st = scores(pun[table[gq, 2 * slot]], qsub[...])
            row = lax.broadcasted_iota(jnp.int32, st.shape, 0)
            live = row < table[gq, 2 * slot + 1]
            total = total + jnp.sum(jnp.where(live, jnp.exp(st), 0.0), axis=0, keepdims=True)
        tot_out[gq, 0:1, rows] = total

        @pl.when(j == NS - 1)
        def _():
            tot_copy(gq).start()

    def step(e, carry):
        s = e // NS
        j = e % NS
        left = z - s
        right = z + s
        from_left = jnp.logical_and(s > 0, left >= 0)
        from_right = jnp.logical_and(s > 0, right < C)

        @pl.when(from_left)
        def _():
            gq = 2 * left + c
            piece(gq, j, right_send, g).wait_recv()

            @pl.when(z + 1 < C)
            def _():
                piece(gq, j, right_send, g + 2).start()

            piece(gq, j, side_send, side).start()

        @pl.when(from_right)
        def _():
            gq = 2 * right + c
            piece(gq, j, left_send, g).wait_recv()

            @pl.when(z > 0)
            def _():
                piece(gq, j, left_send, g - 2).start()

            piece(gq, j, side_send, side).start()

        @pl.loop(0, 4)
        def _(t):
            zq = jnp.where(t % 2 == 0, left, right)
            cq = jnp.where(t < 2, c, 1 - c)
            there = jnp.where(t % 2 == 0, left >= 0, jnp.logical_and(s > 0, right < C))
            there = jnp.logical_and(there, jnp.logical_or(s > 0, t >= 2))
            gq = 2 * zq + cq

            @pl.when(there)
            def _():
                @pl.when(t >= 2)
                def _():
                    piece(gq, j, side_send, g).wait_recv()

                hard(gq, j)

        return carry

    lax.fori_loop(0, C * NS, step, 0)

    for k in range(1, G):
        tot_arrival(lax.rem(g + k, G)).wait_recv()
    total = tot_in[0, 0:1, :]
    for k in range(1, G):
        total = total + tot_in[k, 0:1, :]
    loss = jnp.log(total) - pos
    loss_ref[...] = loss
    w = weights[...]
    lane = lax.broadcasted_iota(jnp.int32, (8, LANES), 1)
    weighted = jnp.sum(w * loss, axis=1, keepdims=True)
    weight = jnp.sum(w, axis=1, keepdims=True)
    part = jnp.where(lane == 0, weighted, jnp.where(lane == 1, weight, 0.0))

    def exchange(axis, me_, n, out, slots, send, rec):
        def copy(k):
            return pltpu.make_async_remote_copy(
                out,
                slots.at[me_],
                send.at[k],
                rec.at[me_],
                device_id={axis: lax.rem(me_ + k, n)},
                device_id_type=MESH,
            )

        def arrival(k):
            src = lax.rem(me_ + k, n)
            return pltpu.make_async_remote_copy(
                out,
                slots.at[src],
                send.at[k],
                rec.at[src],
                device_id={axis: src},
                device_id_type=MESH,
            )

        for k in range(1, n):
            copy(k).start()
        for k in range(1, n):
            arrival(k).wait_recv()
        for k in range(1, n):
            copy(k).wait_send()

    part_out[...] = part
    part_grp[g] = part
    exchange("grp", g, G, part_out, part_grp, grp_send, grp_recv)
    total = part_grp[0]
    for k in range(1, G):
        total = total + part_grp[k]
    sum_out[...] = total
    part_rep[r] = total
    exchange("rep", r, REP, sum_out, part_rep, rep_send, rep_recv)
    total = part_rep[0]
    for k in range(1, REP):
        total = total + part_rep[k]
    mean_ref[...] = jnp.broadcast_to(total[:, 0:1] / total[:, 1:2], mean_ref.shape)

    for k in range(1, G):
        want_copy(k).wait_send()
        tot_copy(lax.rem(g + k, G)).wait_send()

    @pl.loop(0, NS)
    def _(j):
        @pl.when(z + 1 < C)
        def _():
            own_piece(j, right_send, g + 2).wait_send()

        @pl.when(z > 0)
        def _():
            own_piece(j, left_send, g - 2).wait_send()

        own_piece(j, side_send, side).wait_send()

    @pl.loop(NS, C * NS)
    def _(e):
        s = e // NS
        j = e % NS
        left = z - s
        right = z + s

        @pl.when(left >= 0)
        def _():
            gq = 2 * left + c

            @pl.when(z + 1 < C)
            def _():
                piece(gq, j, right_send, g + 2).wait_send()

            piece(gq, j, side_send, side).wait_send()

        @pl.when(right < C)
        def _():
            gq = 2 * right + c

            @pl.when(z > 0)
            def _():
                piece(gq, j, left_send, g - 2).wait_send()

            piece(gq, j, side_send, side).wait_send()


def local(G, REP, queries, passages, counts, positive, neg, weights):
    QG, D = queries.shape
    blocks = counts.shape[0]
    BR = passages.shape[0] // blocks
    NS = QG // LANES
    dma = pltpu.SemaphoreType.DMA
    vmem = pl.BlockSpec(memory_space=pltpu.VMEM)
    smem = pl.BlockSpec(memory_space=pltpu.SMEM)
    hbm = pl.BlockSpec(memory_space=pl.ANY)
    loss, mean = pl.pallas_call(
        functools.partial(kernel, G, REP),
        out_shape=(
            jax.ShapeDtypeStruct((1, QG), jnp.float32),
            jax.ShapeDtypeStruct((8, LANES), jnp.float32),
        ),
        in_specs=[smem, vmem, vmem, vmem, hbm, hbm],
        out_specs=(vmem, vmem),
        scratch_shapes=[
            pltpu.VMEM((G, QG, D), jnp.bfloat16),
            pltpu.VMEM((blocks, BR, D), jnp.bfloat16),
            pltpu.VMEM((QG, D), jnp.bfloat16),
            pltpu.VMEM((LANES, D), jnp.bfloat16),
            pltpu.VMEM((8, LANES), jnp.int32),
            pltpu.VMEM((G, 8, LANES), jnp.int32),
            pltpu.SMEM((G, 8, LANES), jnp.int32),
            pltpu.SMEM((G, 4), jnp.int32),
            pltpu.VMEM((G, 8, QG), jnp.float32),
            pltpu.VMEM((G, 8, QG), jnp.float32),
            pltpu.VMEM((8, LANES), jnp.float32),
            pltpu.VMEM((G, 8, LANES), jnp.float32),
            pltpu.VMEM((8, LANES), jnp.float32),
            pltpu.VMEM((REP, 8, LANES), jnp.float32),
            dma,
            dma((blocks,)),
            dma((G,)),
            dma((G,)),
            dma,
            dma((G, NS)),
            dma((G, NS)),
            dma((G, NS)),
            dma((G, NS)),
            dma((G,)),
            dma((G,)),
            dma((G,)),
            dma((G,)),
            dma((REP,)),
            dma((REP,)),
        ],
        compiler_params=pltpu.CompilerParams(
            collective_id=0, has_side_effects=True, vmem_limit_bytes=62 * 1024 * 1024
        ),
    )(
        counts,
        neg,
        positive.reshape(1, QG),
        weights.reshape(1, QG),
        queries,
        passages.reshape(blocks, BR, D),
    )
    return loss.reshape(QG), mean[0, 0]


def solution(mesh):
    split = P(("grp", "rep"))
    rows = P(("grp", "rep"), None)
    return jax.shard_map(
        functools.partial(local, mesh.shape["grp"], mesh.shape["rep"]),
        mesh=mesh,
        in_specs=(rows, rows, split, split, rows, split),
        out_specs=(split, P()),
        check_vma=False,
    )
```

time: 325 us -> 157 us (0.48)
  waiting for transfers between devices: 213 us -> 0 us
  Pallas kernels: 0 us -> 152 us
  blocking collectives: 38.1 us -> 0 us
  matrix products: 18.4 us -> 0 us
  starting transfers between devices: 16.7 us -> 0 us
  other arithmetic: 16.1 us -> 1.25 us
  local copies, waits for them, and re-layouts: 18.2 us -> 3.71 us
    all_to_all x3 -> x0, waiting for transfers between devices: 213 us -> none  [the longest x1 213 us: local(): lax.all_to_all(picked, 'grp', split_axis=0, concat_axis=0, tiled=True)]
    pallas_call x0 -> x1, Pallas kernels: none -> 152 us  [local(): pl.pallas_call(functools.partial(kernel, G, REP), out_shape=(jax.ShapeDty...]
    psum x1 -> x0, blocking collectives: 38.1 us -> none  [local(): lax.psum((jnp.sum(query_weights * query_loss), jnp.sum(query_weights)), (...]
    dot_general x2 -> x0, matrix products: 18.4 us -> none  [the longest x1 9.91 us: local(): lax.dot_general(question_unit_vectors, document_unit_vectors, (((1,), (1,...]
    all_to_all x3 -> x0, starting transfers between devices: 16.7 us -> none  [the longest x1 6.35 us: local(): lax.all_to_all(requests, 'grp', split_axis=0, concat_axis=0, tiled=True)]
    gather x2 -> x0, local copies, waits for them, and re-layouts: 14.6 us -> none  [the longest x1 9.52 us: local(): picked = unit_blocks[safe_block]]
    reduce_sum x5 -> x0, other arithmetic: 8.36 us -> none  [the longest x2 6.69 us: normalize(): jnp.sum(values * values, axis=-1, keepdims=True) + norm_epsilon]
    convert_element_type x1 -> x0, other arithmetic: 5.5 us -> none  [normalize(): return (values * scale).astype(jnp.bfloat16)]
  transfers between devices with their start and end apart: 3 -> 0, of which waited for: 1 -> 0; matrix products, arithmetic and copies ran while one was open for 11% -> 0% of each run, Pallas kernels for 0% -> 0%
where the time goes in v1:
time: 157 us
  Pallas kernels  152 us (97%)
  local copies, waits for them, and re-layouts  3.71 us (2%)
    pallas_call x1, Pallas kernels, local(): pl.pallas_call(functools.partial(kernel, G, REP), out_shape=(jax.ShapeDty...  152 us

profile of v1, /device:TPU:0, one launch (start us, length us, event | category | flops | bytes accessed | tf_op | source)
XLA Modules:
  0.0 157.2 jit_solution(2223143710000171934)
XLA Ops:
  0.6 1.2 reshape.16.positive
  1.9 1.3 reshape.17.weights
  3.1 151.6 %shard_map.77 = (f32[1,384]{1,0:T(1,128)}, f32[8,128]{1,0:T(8,128)}) custom-call(s32[16]{0:T(128)} %counts.1, s32[1,12]{1,0:T(1,128)} %neg.1, s32[1,384]{1,0:T(1,128)} %reshape.16.positive, f32[1,384]{1,0:T(1,128)} %reshape.17.weights, bf16[384,2560]{1,0:T(8,128)(2,1)} %q_hbm.1, bf16[16,128,2560]{2,1,0:T(8,128)(2,1)} %bitcast.2), custom_call_target="tpu_custom_call" | custom-call | tf_op jit(solution)/shard_map/pallas_call | solution.py:411
  154.8 1.2 slice.3
  156.0 1.2 reduce

commit v2 on v1

--- a/solution.py
+++ b/solution.py
@@ -56,6 +56,10 @@
     part_grp,
     sum_out,
     part_rep,
+    blk_out,
+    blk_in,
+    live_out,
+    live_in,
     q_sem,
     p_sem,
     want_send,
@@ -71,6 +75,10 @@
     grp_recv,
     rep_send,
     rep_recv,
+    blk_send,
+    blk_recv,
+    live_send,
+    live_recv,
 ):
     g = lax.axis_index("grp")
     r = lax.axis_index("rep")
@@ -84,6 +92,23 @@
     c = g % 2
     side = 2 * z + 1 - c
 
+    short = C >= 4
+
+    def by_blocks(owner_z, query_z):
+        if not short:
+            return owner_z < 0
+        return jnp.logical_or(
+            jnp.logical_and(owner_z == 0, query_z == 1),
+            jnp.logical_and(owner_z == C - 1, query_z == C - 2),
+        )
+
+    inner_z = jnp.where(z == 0, 1, C - 2)
+    end_z = jnp.where(z == 1, 0, C - 1)
+    at_end = by_blocks(z, inner_z)
+    by_end = by_blocks(end_z, z)
+    own_right = jnp.logical_and(z + 1 < C, jnp.logical_not(by_blocks(z + 1, z)))
+    own_left = jnp.logical_and(z > 0, jnp.logical_not(by_blocks(z - 1, z)))
+
     barrier = pltpu.get_barrier_semaphore()
     for k in range(1, G):
         pl.semaphore_signal(
@@ -156,11 +181,11 @@
 
     @pl.loop(0, NS)
     def _(j):
-        @pl.when(z + 1 < C)
+        @pl.when(own_right)
         def _():
             own_piece(j, right_send, g + 2).start()
 
-        @pl.when(z > 0)
+        @pl.when(own_left)
         def _():
             own_piece(j, left_send, g - 2).start()
 
@@ -214,6 +239,68 @@
         table[gq, 2] = second
         table[gq, 3] = jnp.where(found > 1, counts[second], 0)
 
+    def blk_copy(t):
+        slot = t // 2
+        cq = t % 2
+        return pltpu.make_async_remote_copy(
+            blk_out.at[cq, slot],
+            blk_in.at[c, slot],
+            blk_send.at[cq, slot],
+            blk_recv.at[c, slot],
+            device_id={"grp": 2 * inner_z + cq},
+            device_id_type=MESH,
+        )
+
+    def live_copy(cq):
+        return pltpu.make_async_remote_copy(
+            live_out.at[cq],
+            live_in.at[c],
+            live_send.at[cq],
+            live_recv.at[c],
+            device_id={"grp": 2 * inner_z + cq},
+            device_id_type=MESH,
+        )
+
+    def blk_arrival(t):
+        slot = t // 2
+        co = t % 2
+        return pltpu.make_async_remote_copy(
+            blk_out.at[co, slot],
+            blk_in.at[co, slot],
+            blk_send.at[co, slot],
+            blk_recv.at[co, slot],
+            device_id={"grp": 2 * end_z + co},
+            device_id_type=MESH,
+        )
+
+    def live_arrival(co):
+        return pltpu.make_async_remote_copy(
+            live_out.at[co],
+            live_in.at[co],
+            live_send.at[co],
+            live_recv.at[co],
+            device_id={"grp": 2 * end_z + co},
+            device_id_type=MESH,
+        )
+
+    @pl.when(at_end)
+    def _():
+        @pl.loop(0, 4)
+        def _(t):
+            slot = t // 2
+            cq = t % 2
+            gq = 2 * inner_z + cq
+            blk_out[cq, slot] = pun[table[gq, 2 * slot]]
+            live_out[cq, slot] = jnp.full((8, QG), table[gq, 2 * slot + 1], jnp.int32)
+
+        @pl.loop(0, 2)
+        def _(cq):
+            live_copy(cq).start()
+
+        @pl.loop(0, 4)
+        def _(t):
+            blk_copy(t).start()
+
     def tot_copy(gq):
         return pltpu.make_async_remote_copy(
             tot_out.at[gq],
@@ -249,13 +336,16 @@
         def _():
             tot_copy(gq).start()
 
-    def step(e, carry):
+    def sources(e):
         s = e // NS
-        j = e % NS
         left = z - s
         right = z + s
-        from_left = jnp.logical_and(s > 0, left >= 0)
-        from_right = jnp.logical_and(s > 0, right < C)
+        from_left = jnp.logical_and(left >= 0, jnp.logical_not(by_blocks(z, left)))
+        from_right = jnp.logical_and(right < C, jnp.logical_not(by_blocks(z, right)))
+        return s, e % NS, left, right, from_left, from_right
+
+    def forward(e):
+        s, j, left, right, from_left, from_right = sources(e)
 
         @pl.when(from_left)
         def _():
@@ -279,11 +369,25 @@
 
             piece(gq, j, side_send, side).start()
 
+    @pl.loop(0, C * NS)
+    def _(e):
+        if C > 1:
+
+            @pl.when(jnp.logical_or(e == 0, e > NS))
+            def _():
+                forward(jnp.where(e == 0, NS, e))
+
+        s, j, left, right, from_left, from_right = sources(e)
+
         @pl.loop(0, 4)
         def _(t):
-            zq = jnp.where(t % 2 == 0, left, right)
+            is_left = t % 2 == 0
+            zq = jnp.where(is_left, left, right)
             cq = jnp.where(t < 2, c, 1 - c)
-            there = jnp.where(t % 2 == 0, left >= 0, jnp.logical_and(s > 0, right < C))
+            there = jnp.logical_or(
+                jnp.logical_and(is_left, from_left),
+                jnp.logical_and(jnp.logical_and(t % 2 == 1, s > 0), from_right),
+            )
             there = jnp.logical_and(there, jnp.logical_or(s > 0, t >= 2))
             gq = 2 * zq + cq
 
@@ -295,12 +399,33 @@
 
                 hard(gq, j)
 
-        return carry
-
-    lax.fori_loop(0, C * NS, step, 0)
-
-    for k in range(1, G):
-        tot_arrival(lax.rem(g + k, G)).wait_recv()
+    @pl.when(by_end)
+    def _():
+        @pl.loop(0, 2)
+        def _(co):
+            live_arrival(co).wait_recv()
+            tot_in[2 * end_z + co] = jnp.zeros((8, QG), jnp.float32)
+
+        @pl.loop(0, 4)
+        def _(t):
+            slot = t // 2
+            co = t % 2
+            blk_arrival(t).wait_recv()
+            st = scores(blk_in[co, slot], qown[...])
+            row = lax.broadcasted_iota(jnp.int32, st.shape, 0)
+            live = row < live_in[co, slot, 0:1, :]
+            tot_in[2 * end_z + co, 0:1, :] += jnp.sum(
+                jnp.where(live, jnp.exp(st), 0.0), axis=0, keepdims=True
+            )
+
+    @pl.loop(1, G)
+    def _(k):
+        src = lax.rem(g + k, G)
+
+        @pl.when(jnp.logical_not(by_blocks(src // 2, z)))
+        def _():
+            tot_arrival(src).wait_recv()
+
     total = tot_in[0, 0:1, :]
     for k in range(1, G):
         total = total + tot_in[k, 0:1, :]
@@ -357,15 +482,32 @@
 
     for k in range(1, G):
         want_copy(k).wait_send()
-        tot_copy(lax.rem(g + k, G)).wait_send()
+
+    @pl.loop(1, G)
+    def _(k):
+        dst = lax.rem(g + k, G)
+
+        @pl.when(jnp.logical_not(by_blocks(z, dst // 2)))
+        def _():
+            tot_copy(dst).wait_send()
+
+    @pl.when(at_end)
+    def _():
+        @pl.loop(0, 2)
+        def _(cq):
+            live_copy(cq).wait_send()
+
+        @pl.loop(0, 4)
+        def _(t):
+            blk_copy(t).wait_send()
 
     @pl.loop(0, NS)
     def _(j):
-        @pl.when(z + 1 < C)
+        @pl.when(own_right)
         def _():
             own_piece(j, right_send, g + 2).wait_send()
 
-        @pl.when(z > 0)
+        @pl.when(own_left)
         def _():
             own_piece(j, left_send, g - 2).wait_send()
 
@@ -373,12 +515,9 @@
 
     @pl.loop(NS, C * NS)
     def _(e):
-        s = e // NS
-        j = e % NS
-        left = z - s
-        right = z + s
-
-        @pl.when(left >= 0)
+        _, j, left, right, from_left, from_right = sources(e)
+
+        @pl.when(from_left)
         def _():
             gq = 2 * left + c
 
@@ -388,7 +527,7 @@
 
             piece(gq, j, side_send, side).wait_send()
 
-        @pl.when(right < C)
+        @pl.when(from_right)
         def _():
             gq = 2 * right + c
 
@@ -431,6 +570,10 @@
             pltpu.VMEM((G, 8, LANES), jnp.float32),
             pltpu.VMEM((8, LANES), jnp.float32),
             pltpu.VMEM((REP, 8, LANES), jnp.float32),
+            pltpu.VMEM((2, 2, BR, D), jnp.bfloat16),
+            pltpu.VMEM((2, 2, BR, D), jnp.bfloat16),
+            pltpu.VMEM((2, 2, 8, QG), jnp.int32),
+            pltpu.VMEM((2, 2, 8, QG), jnp.int32),
             dma,
             dma((blocks,)),
             dma((G,)),
@@ -446,6 +589,10 @@
             dma((G,)),
             dma((REP,)),
             dma((REP,)),
+            dma((2, 2)),
+            dma((2, 2)),
+            dma((2,)),
+            dma((2,)),
         ],
         compiler_params=pltpu.CompilerParams(
             collective_id=0, has_side_effects=True, vmem_limit_bytes=62 * 1024 * 1024

time: 157 us -> 131 us (0.83)
  Pallas kernels: 152 us -> 125 us
    pallas_call x1, Pallas kernels: 152 us -> 125 us  [local(): pl.pallas_call(functools.partial(kernel, G, REP), out_shape=(jax.ShapeDty...]
where the time goes in v2:
time: 131 us
  Pallas kernels  125 us (95%)
  local copies, waits for them, and re-layouts  3.71 us (3%)
    pallas_call x1, Pallas kernels, local(): pl.pallas_call(functools.partial(kernel, G, REP), out_shape=(jax.ShapeDty...  125 us

profile of v2, /device:TPU:0, one launch (start us, length us, event | category | flops | bytes accessed | tf_op | source)
XLA Modules:
  0.0 131.0 jit_solution(10575721746809179606)
XLA Ops:
  0.6 1.2 reshape.16.positive
  1.9 1.3 reshape.17.weights
  3.1 125.4 %shard_map.77 = (f32[1,384]{1,0:T(1,128)}, f32[8,128]{1,0:T(8,128)}) custom-call(s32[16]{0:T(128)} %counts.1, s32[1,12]{1,0:T(1,128)} %neg.1, s32[1,384]{1,0:T(1,128)} %reshape.16.positive, f32[1,384]{1,0:T(1,128)} %reshape.17.weights, bf16[384,2560]{1,0:T(8,128)(2,1)} %q_hbm.1, bf16[16,128,2560]{2,1,0:T(8,128)(2,1)} %bitcast.2), custom_call_target="tpu_custom_call" | custom-call | tf_op jit(solution)/shard_map/pallas_call | solution.py:550
  128.6 1.2 slice.3
  129.8 1.2 reduce

commit v3 on v2

--- a/solution.py
+++ b/solution.py
@@ -10,6 +10,8 @@
 sharpness = 20.0
 norm_epsilon = 1e-06
 LANES = 128
+PIECE = 64
+WINDOW = 2
 MESH = pl.DeviceIdType.MESH
 
 
@@ -87,6 +89,10 @@
     listed = neg.shape[1]
     R = LANES
     NS = QG // R
+    T = PIECE if R % PIECE == 0 else R
+    NT = QG // T
+    per = R // T
+    W = min(WINDOW, NT)
     C = G // 2
     z = g // 2
     c = g % 2
@@ -155,7 +161,7 @@
         )
 
     def own_piece(j, sem, target):
-        rows = pl.ds(pl.multiple_of(j * R, R), R)
+        rows = pl.ds(pl.multiple_of(j * T, T), T)
         return pltpu.make_async_remote_copy(
             q_hbm.at[rows],
             qall.at[g, rows],
@@ -166,7 +172,7 @@
         )
 
     def piece(gq, j, sem, target):
-        rows = pl.ds(pl.multiple_of(j * R, R), R)
+        rows = pl.ds(pl.multiple_of(j * T, T), T)
         return pltpu.make_async_remote_copy(
             qall.at[gq, rows],
             qall.at[gq, rows],
@@ -179,17 +185,113 @@
     for k in range(1, G):
         want_copy(k).start()
 
-    @pl.loop(0, NS)
+    right_skip = jnp.where(own_right, W, NT)
+    left_skip = jnp.where(own_left, W, NT)
+
+    def comes_from_left(e):
+        left = z - e // NT
+        return jnp.logical_and(
+            e >= NT, jnp.logical_and(left >= 0, jnp.logical_not(by_blocks(z, left)))
+        )
+
+    def comes_from_right(e):
+        right = z + e // NT
+        return jnp.logical_and(
+            e >= NT, jnp.logical_and(right < C, jnp.logical_not(by_blocks(z, right)))
+        )
+
+    def goes_right(e):
+        own = jnp.logical_and(own_right, jnp.logical_and(e >= 0, e < NT))
+        return jnp.logical_or(own, jnp.logical_and(z + 1 < C, comes_from_left(e)))
+
+    def goes_left(e):
+        own = jnp.logical_and(own_left, jnp.logical_and(e >= 0, e < NT))
+        return jnp.logical_or(own, jnp.logical_and(z > 0, comes_from_right(e)))
+
+    def right_sent(e):
+        @pl.when(goes_right(e))
+        def _():
+            piece(2 * (z - e // NT) + c, e % NT, right_send, g + 2).wait_send()
+
+    def left_sent(e):
+        @pl.when(goes_left(e))
+        def _():
+            piece(2 * (z + e // NT) + c, e % NT, left_send, g - 2).wait_send()
+
+    def send_own(n):
+        @pl.when(own_right)
+        def _():
+            own_piece(n, right_send, g + 2).start()
+
+        @pl.when(own_left)
+        def _():
+            own_piece(n, left_send, g - 2).start()
+
+    def move_right(n):
+        e = n + right_skip
+
+        @pl.when(jnp.logical_and(own_right, e < NT))
+        def _():
+            right_sent(e - W)
+            own_piece(e, right_send, g + 2).start()
+
+        @pl.when(comes_from_left(e))
+        def _():
+            gq = 2 * (z - e // NT) + c
+            j = e % NT
+            piece(gq, j, right_send, g).wait_recv()
+
+            @pl.when(z + 1 < C)
+            def _():
+                right_sent(e - W)
+                piece(gq, j, right_send, g + 2).start()
+
+            piece(gq, j, side_send, side).start()
+
+    def move_left(n):
+        e = n + left_skip
+
+        @pl.when(jnp.logical_and(own_left, e < NT))
+        def _():
+            left_sent(e - W)
+            own_piece(e, left_send, g - 2).start()
+
+        @pl.when(comes_from_right(e))
+        def _():
+            gq = 2 * (z + e // NT) + c
+            j = e % NT
+            piece(gq, j, left_send, g).wait_recv()
+
+            @pl.when(z > 0)
+            def _():
+                left_sent(e - W)
+                piece(gq, j, left_send, g - 2).start()
+
+            piece(gq, j, side_send, side).start()
+
+    def tick(n):
+        @pl.loop(0, 2)
+        def _(t):
+            to_right = jnp.logical_xor(t == 1, own_right)
+
+            @pl.when(to_right)
+            def _():
+                move_right(n)
+
+            @pl.when(jnp.logical_not(to_right))
+            def _():
+                move_left(n)
+
+    for n in range(W):
+        send_own(n)
+
+    @pl.loop(0, NT)
     def _(j):
-        @pl.when(own_right)
-        def _():
-            own_piece(j, right_send, g + 2).start()
-
-        @pl.when(own_left)
-        def _():
-            own_piece(j, left_send, g - 2).start()
-
         own_piece(j, side_send, side).start()
+
+    stride = max(1, blocks // max(1, NT - W))
+    early = blocks // stride
+    early = min(early, NT)
 
     own_copy.wait()
 
@@ -206,8 +308,13 @@
         row = lax.broadcasted_iota(jnp.int32, st.shape, 0)
         live = row < counts[b]
         total = total + jnp.sum(jnp.where(live, jnp.exp(st), 0.0), axis=0, keepdims=True)
-        hit = row + b * BR == positive[...]
+        hit = row + b * BR == positive[...].reshape(1, QG)
         pos = pos + jnp.sum(jnp.where(hit, st, 0.0), axis=0, keepdims=True)
+
+        @pl.when(jnp.logical_and(b % stride == stride - 1, b // stride < early))
+        def _():
+            tick(b // stride)
+
         return total, pos
 
     zero = jnp.zeros((1, QG), jnp.float32)
@@ -336,60 +443,21 @@
         def _():
             tot_copy(gq).start()
 
-    def sources(e):
-        s = e // NS
-        left = z - s
-        right = z + s
-        from_left = jnp.logical_and(left >= 0, jnp.logical_not(by_blocks(z, left)))
-        from_right = jnp.logical_and(right < C, jnp.logical_not(by_blocks(z, right)))
-        return s, e % NS, left, right, from_left, from_right
-
-    def forward(e):
-        s, j, left, right, from_left, from_right = sources(e)
-
-        @pl.when(from_left)
-        def _():
-            gq = 2 * left + c
-            piece(gq, j, right_send, g).wait_recv()
-
-            @pl.when(z + 1 < C)
-            def _():
-                piece(gq, j, right_send, g + 2).start()
-
-            piece(gq, j, side_send, side).start()
-
-        @pl.when(from_right)
-        def _():
-            gq = 2 * right + c
-            piece(gq, j, left_send, g).wait_recv()
-
-            @pl.when(z > 0)
-            def _():
-                piece(gq, j, left_send, g - 2).start()
-
-            piece(gq, j, side_send, side).start()
-
-    @pl.loop(0, C * NS)
-    def _(e):
-        if C > 1:
-
-            @pl.when(jnp.logical_or(e == 0, e > NS))
-            def _():
-                forward(jnp.where(e == 0, NS, e))
-
-        s, j, left, right, from_left, from_right = sources(e)
+    def compute(n):
+        e_right = n + right_skip
+        e_left = n + left_skip
 
         @pl.loop(0, 4)
         def _(t):
             is_left = t % 2 == 0
-            zq = jnp.where(is_left, left, right)
-            cq = jnp.where(t < 2, c, 1 - c)
+            e = jnp.where(is_left, e_right, e_left)
+            zq = jnp.where(is_left, z - e // NT, z + e // NT)
+            j = e % NT
             there = jnp.logical_or(
-                jnp.logical_and(is_left, from_left),
-                jnp.logical_and(jnp.logical_and(t % 2 == 1, s > 0), from_right),
+                jnp.logical_and(is_left, comes_from_left(e)),
+                jnp.logical_and(t % 2 == 1, comes_from_right(e)),
             )
-            there = jnp.logical_and(there, jnp.logical_or(s > 0, t >= 2))
-            gq = 2 * zq + cq
+            gq = 2 * zq + jnp.where(t < 2, c, 1 - c)
 
             @pl.when(there)
             def _():
@@ -397,7 +465,33 @@
                 def _():
                     piece(gq, j, side_send, g).wait_recv()
 
-                hard(gq, j)
+                @pl.when(j % per == per - 1)
+                def _():
+                    hard(gq, j // per)
+
+    @pl.loop(early, C * NT + early)
+    def _(n):
+        @pl.when(n < C * NT)
+        def _():
+            tick(n)
+
+        caught_up = n >= 2 * early
+        first = jnp.where(caught_up, n, 2 * (n - early))
+        last = jnp.where(caught_up, n, first + 1)
+
+        @pl.loop(first, last + 1)
+        def _(m):
+            @pl.when(m < C * NT)
+            def _():
+                compute(m)
+
+        j = n - 2 * early
+
+        @pl.when(jnp.logical_and(j >= 0, j < NS))
+        def _():
+            for i in range(per):
+                piece(side, j * per + i, side_send, g).wait_recv()
+            hard(side, j)
 
     @pl.when(by_end)
     def _():
@@ -430,8 +524,8 @@
     for k in range(1, G):
         total = total + tot_in[k, 0:1, :]
     loss = jnp.log(total) - pos
-    loss_ref[...] = loss
-    w = weights[...]
+    loss_ref[...] = loss.reshape(QG)
+    w = weights[...].reshape(1, QG)
     lane = lax.broadcasted_iota(jnp.int32, (8, LANES), 1)
     weighted = jnp.sum(w * loss, axis=1, keepdims=True)
     weight = jnp.sum(w, axis=1, keepdims=True)
@@ -478,7 +572,7 @@
     total = part_rep[0]
     for k in range(1, REP):
         total = total + part_rep[k]
-    mean_ref[...] = jnp.broadcast_to(total[:, 0:1] / total[:, 1:2], mean_ref.shape)
+    mean_ref[...] = total[0:1, 0:1] / total[0:1, 1:2]
 
     for k in range(1, G):
         want_copy(k).wait_send()
@@ -501,48 +595,39 @@
         def _(t):
             blk_copy(t).wait_send()
 
-    @pl.loop(0, NS)
+    @pl.loop(0, NT)
     def _(j):
-        @pl.when(own_right)
-        def _():
-            own_piece(j, right_send, g + 2).wait_send()
-
-        @pl.when(own_left)
-        def _():
-            own_piece(j, left_send, g - 2).wait_send()
-
         own_piece(j, side_send, side).wait_send()
 
-    @pl.loop(NS, C * NS)
+    @pl.loop(0, C * NT)
+    def _(n):
+        e_right = n + right_skip
+        e_left = n + left_skip
+
+        @pl.when(comes_from_left(e_right))
+        def _():
+            piece(2 * (z - e_right // NT) + c, e_right % NT, side_send, side).wait_send()
+
+        @pl.when(comes_from_right(e_left))
+        def _():
+            piece(2 * (z + e_left // NT) + c, e_left % NT, side_send, side).wait_send()
+
+    @pl.loop(0, C * NT)
     def _(e):
-        _, j, left, right, from_left, from_right = sources(e)
-
-        @pl.when(from_left)
-        def _():
-            gq = 2 * left + c
-
-            @pl.when(z + 1 < C)
-            def _():
-                piece(gq, j, right_send, g + 2).wait_send()
-
-            piece(gq, j, side_send, side).wait_send()
-
-        @pl.when(from_right)
-        def _():
-            gq = 2 * right + c
-
-            @pl.when(z > 0)
-            def _():
-                piece(gq, j, left_send, g - 2).wait_send()
-
-            piece(gq, j, side_send, side).wait_send()
+        @pl.when(jnp.logical_not(goes_right(e + W)))
+        def _():
+            right_sent(e)
+
+        @pl.when(jnp.logical_not(goes_left(e + W)))
+        def _():
+            left_sent(e)
 
 
 def local(G, REP, queries, passages, counts, positive, neg, weights):
     QG, D = queries.shape
     blocks = counts.shape[0]
     BR = passages.shape[0] // blocks
-    NS = QG // LANES
+    NT = QG // (PIECE if LANES % PIECE == 0 else LANES)
     dma = pltpu.SemaphoreType.DMA
     vmem = pl.BlockSpec(memory_space=pltpu.VMEM)
     smem = pl.BlockSpec(memory_space=pltpu.SMEM)
@@ -550,8 +635,8 @@
     loss, mean = pl.pallas_call(
         functools.partial(kernel, G, REP),
         out_shape=(
-            jax.ShapeDtypeStruct((1, QG), jnp.float32),
-            jax.ShapeDtypeStruct((8, LANES), jnp.float32),
+            jax.ShapeDtypeStruct((QG,), jnp.float32),
+            jax.ShapeDtypeStruct((1, 1), jnp.float32),
         ),
         in_specs=[smem, vmem, vmem, vmem, hbm, hbm],
         out_specs=(vmem, vmem),
@@ -579,10 +664,10 @@
             dma((G,)),
             dma((G,)),
             dma,
-            dma((G, NS)),
-            dma((G, NS)),
-            dma((G, NS)),
-            dma((G, NS)),
+            dma((G, NT)),
+            dma((G, NT)),
+            dma((G, NT)),
+            dma((G, NT)),
             dma((G,)),
             dma((G,)),
             dma((G,)),
@@ -600,12 +685,12 @@
     )(
         counts,
         neg,
-        positive.reshape(1, QG),
-        weights.reshape(1, QG),
+        positive,
+        weights,
         queries,
         passages.reshape(blocks, BR, D),
     )
-    return loss.reshape(QG), mean[0, 0]
+    return loss, mean.reshape(())
 
 
 def solution(mesh):

time: 131 us -> 127 us (0.969)
  local copies, waits for them, and re-layouts: 3.71 us -> 1.25 us
  Pallas kernels: 125 us -> 123 us
  between operations: 0.64 us -> 2.4 us
    reshape x2 -> x0, local copies, waits for them, and re-layouts: 2.51 us -> none  [the longest x1 1.27 us: local(): weights.reshape(1, QG)]
    pallas_call x1, Pallas kernels: 125 us -> 123 us  [local(): pl.pallas_call(functools.partial(kernel, G, REP), out_shape=(jax.ShapeDty...]
where the time goes in v3:
time: 127 us
  Pallas kernels  123 us (97%)
  between operations  2.4 us (2%)
    pallas_call x1, Pallas kernels, local(): pl.pallas_call(functools.partial(kernel, G, REP), out_shape=(jax.ShapeDty...  123 us

profile of v3, /device:TPU:0, one launch (start us, length us, event | category | flops | bytes accessed | tf_op | source)
XLA Modules:
  0.0 126.8 jit_solution(3989208821308597582)
XLA Ops:
  0.6 123.1 %shard_map.77 = (f32[384]{0:T(512)}, f32[1,1]{1,0:T(1,128)}) custom-call(s32[16]{0:T(128)} %counts.1, s32[1,12]{1,0:T(1,128)} %neg.1, s32[384]{0:T(512)} %positive.1, f32[384]{0:T(512)} %weights.1, bf16[384,2560]{1,0:T(8,128)(2,1)} %q_hbm.1, bf16[16,128,2560]{2,1,0:T(8,128)(2,1)} %bitcast.2), custom_call_target="tpu_custom_call" | custom-call | tf_op jit(solution)/shard_map/pallas_call | solution.py:635
  123.7 1.2 copy.10
